TPU v7x, 32 devices: a whole 2x2x4 slice. The times are simulated.
32 devices in a mesh: groups: 2 (over y), hid: 8 (over z, x), row: 2 (over core).
Axes of the slice: x: 2, y: 2, z: 4, core: 2. Of those that a mesh axis runs over, the one named last changes fastest.
Arguments:
- gate_proj: bfloat16 [32, 32768], P(('groups', 'row'), 'hid'), parts along dimension 0, may hold values from -6 to 6
- up_proj: bfloat16 [32, 32768], P(('groups', 'row'), 'hid'), parts along dimension 0, may hold values from -6 to 6
- hadamard_signs: int32 [32768], P('hid'), may hold values from 0 to 1
- down_codes: bfloat16 [32768, 8192], P('hid', 'row'), may hold values from -127 to 127, as said below
- down_scales: int32 [8192], P('row'), may hold values from 128 to 1279
- residual: bfloat16 [32, 8192], P(('groups', 'hid'), 'row'), parts along dimension 0, may hold values from -16 to 16
- norm_gain: bfloat16 [8192], P('row'), may hold values from 0.099609375 to 1.8984375
- qkv_codes: bfloat16 [8192, 18432], P('row', 'hid'), may hold values from -127 to 127, as said below
- qkv_scales: int32 [18432], P('hid'), may hold values from 128 to 1279
Outputs:
- new_stream: bfloat16 [32, 8192], P(('groups', 'hid'), 'row'), parts along dimension 0
- joined_qkv: bfloat16 [32, 18432], P(('groups', 'row'), 'hid'), parts along dimension 0
There are 2 independent parts, one for each index of `groups`. A program takes and returns all parts, laid end to end along the dimension named above; an argument that names none is the same for every part. Nothing has to cross between parts.
Inputs may be any that keep to these rules, and one draw needn't show every extreme that they name: `down_codes`: every entry is a whole number. `qkv_codes`: every entry is a whole number.
All inputs are finite; a program needn't handle non-finite values.
Results may differ from a plain program's by a relative error of at most 0.0062.
Values may be sent and summed in bfloat16 or wider, within the bound.
A program may use at most 128 MiB of HBM per device.

v0:
```python
import math

import jax
import jax.numpy as jnp
from jax import lax
from jax.sharding import PartitionSpec as P

epsilon = 1e-05


def partner_2(block, axis, bit):
    count = lax.axis_size(axis)
    route = []
    for low in range(count):
        high = low | 1 << bit
        if high != low and high < count:
            route += [(low, high), (high, low)]
    return lax.ppermute(block, axis, route)


def sylvester(order_size):
    row_index = lax.broadcasted_iota(jnp.int32, (order_size, order_size), 0)
    column_index = lax.broadcasted_iota(jnp.int32, (order_size, order_size), 1)
    result = jnp.ones((order_size, order_size), jnp.float32)
    for bit_number in range(order_size.bit_length() - 1):
        both_set = row_index // 2**bit_number % 2 * (column_index // 2**bit_number % 2)
        result = result * (1.0 - 2.0 * both_set.astype(jnp.float32))
    return result


def factor_list(length):
    factors = []
    remain = length
    while remain > 1:
        factor = min(remain, 128)
        factors.append(factor)
        remain = remain // factor
    return factors


def transform_axis(values, order_size, axis_place):
    product_moved = jnp.tensordot(
        values, sylvester(order_size), axes=([axis_place], [0]), precision=lax.Precision.HIGHEST
    )
    return jnp.moveaxis(product_moved, -1, axis_place)


def transform_last(values):
    factors = factor_list(values.shape[-1])
    leading = values.shape[:-1]
    shaped = values.reshape(leading + tuple(factors))
    for offset, order_size in enumerate(factors):
        shaped = transform_axis(shaped, order_size, len(leading) + offset)
    return shaped.reshape(values.shape)


def body(
    gate_proj,
    up_proj,
    hadamard_signs,
    down_codes,
    down_scales,
    residual,
    norm_gain,
    qkv_codes,
    qkv_scales,
):
    hidden = (jax.nn.silu(gate_proj.astype(jnp.float32)) * up_proj.astype(jnp.float32)).astype(
        jnp.bfloat16
    )
    flips = (1 - 2 * hadamard_signs).astype(jnp.bfloat16)
    signed = hidden * flips[None, :]
    groups = lax.axis_size("hid")
    local_rows, local_width = signed.shape
    norm_factor = 1.0 / math.sqrt(local_width * groups)
    mixed = transform_last(signed.astype(jnp.float32))
    position = lax.axis_index("hid")
    for bit_number in range(groups.bit_length() - 1):
        partner = partner_2(mixed, "hid", bit_number)
        upper_half = position // 2**bit_number % 2 == 1
        mixed = jnp.where(upper_half, partner - mixed, mixed + partner)
    rotated = (mixed * norm_factor).astype(jnp.bfloat16)
    partial_value = jnp.dot(
        lax.all_gather(rotated, "row", axis=0, tiled=True),
        down_codes,
        preferred_element_type=jnp.float32,
    )
    column_scale = (down_scales.astype(jnp.float32) * 2.0 ** (-23))[None, :]
    own_rows = residual.shape[0]
    every_residual = lax.all_gather(residual, "hid", axis=0, tiled=True)
    summed = lax.psum(partial_value, "hid")
    stream_all = (every_residual.astype(jnp.float32) + summed * column_scale).astype(jnp.bfloat16)
    new_stream = lax.dynamic_slice_in_dim(stream_all, lax.axis_index("hid") * own_rows, own_rows, 0)
    stream_wide = stream_all.astype(jnp.float32)
    scaled_rows = (stream_wide * norm_gain.astype(jnp.float32)[None, :]).astype(jnp.bfloat16)
    squares = jnp.sum(stream_wide * stream_wide, axis=1)
    out_rows = stream_all.shape[0] // lax.axis_size("row")
    full_width = stream_all.shape[1] * lax.axis_size("row")
    projected = lax.psum_scatter(
        jnp.dot(scaled_rows, qkv_codes, preferred_element_type=jnp.float32),
        "row",
        scatter_dimension=0,
        tiled=True,
    )
    all_squares = lax.psum(squares, "row")
    row_squares = lax.dynamic_slice_in_dim(
        all_squares, lax.axis_index("row") * out_rows, out_rows, 0
    )
    inverse = lax.rsqrt(row_squares / full_width + epsilon)
    output_scale = (qkv_scales.astype(jnp.float32) * 2.0 ** (-22))[None, :]
    joined_qkv = (projected * inverse[:, None] * output_scale).astype(jnp.bfloat16)
    return (new_stream, joined_qkv)


def solution(mesh):
    return jax.shard_map(
        body,
        mesh=mesh,
        in_specs=(
            P(("groups", "row"), "hid"),
            P(("groups", "row"), "hid"),
            P("hid"),
            P("hid", "row"),
            P("row"),
            P(("groups", "hid"), "row"),
            P("row"),
            P("row", "hid"),
            P("hid"),
        ),
        out_specs=(P(("groups", "hid"), "row"), P(("groups", "row"), "hid")),
        check_vma=False,
    )
```

profile of v0, /device:TPU:0, one launch (start us, length us, event | category | flops | bytes accessed | tf_op | source)
XLA Modules:
  0.0 144.5 jit_solution(14292946847741064035)
XLA Ops:
  7.2 0.0 copy-start
  7.2 0.0 copy-start.2
  7.2 0.0 copy-start.1
  7.2 0.0 all-reduce.2.cloned.1.call-start
  7.4 0.7 subtract_convert_fusion
  8.1 0.9 fusion.68
  9.1 0.2 reshape.15
  9.3 0.7 convolution_bitcast_fusion
  10.0 1.1 fusion.161
  11.0 0.2 reshape.16
  11.3 3.0 %collective-permute-start = (f32[8,4096]{1,0:T(8,128)S(1)}, f32[8,4096]{1,0:T(8,128)S(1)}, u32[]{:S(2)}, u32[]{:S(2)}) collective-permute-start(f32[8,4096]{1,0:T(8,128)S(1)} %reshape.16), channel_id=1, source_target_pairs={{0,2},{2,0},{4,6},{6,4},{8,10},{10,8},{12,14},{14,12},{1,3},{3,1},... | collective-permute-start | bytes 393224 | tf_op jit(solution)/shard_map/ppermute | solution.py:18
  14.3 3.5 %collective-permute-done = f32[8,4096]{1,0:T(8,128)S(1)} collective-permute-done((f32[8,4096]{1,0:T(8,128)S(1)}, f32[8,4096]{1,0:T(8,128)S(1)}, u32[]{:S(2)}, u32[]{:S(2)}) %collective-permute-start) | collective-permute-done | bytes 131104 | tf_op jit(solution)/shard_map/ppermute | solution.py:18
  17.8 1.9 %collective-permute-start.1 = (f32[8,4096]{1,0:T(8,128)S(1)}, f32[8,4096]{1,0:T(8,128)S(1)}, u32[]{:S(2)}, u32[]{:S(2)}) collective-permute-start(f32[8,4096]{1,0:T(8,128)S(1)} %add_select_fusion.1), channel_id=1, source_target_pairs={{0,4},{4,0},{2,6},{6,2},{8,12},{12,8},{10,14},{14,10},{1,5},{5,1},... | collective-permute-start | bytes 393224 | tf_op jit(solution)/shard_map/ppermute | solution.py:18
  19.7 3.1 %collective-permute-done.1 = f32[8,4096]{1,0:T(8,128)S(1)} collective-permute-done((f32[8,4096]{1,0:T(8,128)S(1)}, f32[8,4096]{1,0:T(8,128)S(1)}, u32[]{:S(2)}, u32[]{:S(2)}) %collective-permute-start.1) | collective-permute-done | bytes 131104 | tf_op jit(solution)/shard_map/ppermute | solution.py:18
  22.9 2.9 %collective-permute-start.2 = (f32[8,4096]{1,0:T(8,128)S(1)}, f32[8,4096]{1,0:T(8,128)S(1)}, u32[]{:S(2)}, u32[]{:S(2)}) collective-permute-start(f32[8,4096]{1,0:T(8,128)S(1)} %add_select_fusion), channel_id=1, source_target_pairs={{0,8},{8,0},{2,10},{10,2},{4,12},{12,4},{6,14},{14,6},{1,9},{9,1},... | collective-permute-start | bytes 393224 | tf_op jit(solution)/shard_map/ppermute | solution.py:18
  25.8 0.7 convert_multiply_fusion.4
  26.5 3.7 %collective-permute-done.2 = f32[8,4096]{1,0:T(8,128)S(1)} collective-permute-done((f32[8,4096]{1,0:T(8,128)S(1)}, f32[8,4096]{1,0:T(8,128)S(1)}, u32[]{:S(2)}, u32[]{:S(2)}) %collective-permute-start.2) | collective-permute-done | bytes 131104 | tf_op jit(solution)/shard_map/ppermute | solution.py:18
  30.3 1.9 %all_gather.7 = bf16[16,4096]{1,0:T(8,128)(2,1)S(1)} all-gather(bf16[8,4096]{1,0:T(8,128)(2,1)S(1)} %multiply_convert_fusion), channel_id=1, replica_groups=mesh['groups'=2,'hid'=8,'row'=2] {'row'}, dimensions={0}, use_global_device_ids=true | all-gather | bytes 196608 | tf_op jit(solution)/shard_map/all_gather | solution.py:84
  32.2 13.5 %fusion.266 = f32[16,4096]{1,0:T(8,128)} fusion(bf16[16,4096]{1,0:T(8,128)(2,1)S(1)} %all_gather.7, bf16[4096,4096]{1,0:T(8,128)(2,1)} %param.12), kind=kOutput, calls=%fused_computation.410 | convolution fusion | flops 536870912 | bytes 33947648 | tf_op jit(solution)/shard_map/dot_general | solution.py:83
  45.7 0.0 all-reduce.2.cloned.1.call-update
  45.7 0.0 reduce-scatter.2.cloned.1.call-start
  45.8 0.0 copy-done
  45.8 31.1 %all-gather = bf16[8,2,4096]{2,1,0:T(2,128)(2,1)S(1)} all-gather(bf16[1,2,4096]{2,1,0:T(2,128)(2,1)S(1)} %bitcast.14), channel_id=1, replica_groups=mesh['groups'=2,'hid'=8,'row'=2] {'hid'}, dimensions={0}, use_global_device_ids=true | all-gather | bytes 147456 | tf_op jit(solution)/shard_map/all_gather | solution.py:90
  76.9 41.4 %all-reduce.2.cloned.1.call-done = f32[16,4096]{1,0:T(8,128)} async-done(((f32[16,4096]{1,0:T(8,128)}), f32[16,4096]{1,0:T(8,128)}) %all-reduce.2.cloned.1.call-update) | async-done | bytes 262160 | tf_op jit(solution)/shard_map/psum | solution.py:91
  118.4 1.1 fusion.1
  119.5 9.6 %fusion.6 = f32[16,2304]{1,0:T(8,128)} fusion(bf16[4096,2304]{1,0:T(8,128)(2,1)} %param.16, bf16[16,4096]{1,0:T(8,128)(2,1)S(1)} %get-tuple-element.3, f32[4096]{0:T(1024)S(1)} %convert_element_type.97), kind=kOutput, calls=%fused_computation.12 | convolution fusion | flops 302186496 | bytes 19169280 | tf_op jit(solution)/shard_map/dot_general | solution.py:100
  129.0 0.0 reduce-scatter.2.cloned.1.call-update
  129.1 2.5 %psum.15 = f32[16]{0:T(128)S(1)} all-reduce(f32[16]{0:T(128)S(1)} %get-tuple-element.2), channel_id=1, replica_groups=mesh['groups'=2,'hid'=8,'row'=2] {'row'}, use_global_device_ids=true, to_apply=%region_3.4 | all-reduce | flops 16 | bytes 128 | tf_op jit(solution)/shard_map/psum | solution.py:105
  131.5 0.1 add_rsqrt_fusion
  131.6 0.6 constant_dynamic-slice_fusion
  132.3 3.8 %reduce-scatter.2.cloned.1.call-done = f32[8,2304]{1,0:T(8,128)} async-done(((f32[16,2304]{1,0:T(8,128)}), f32[8,2304]{1,0:T(8,128)}) %reduce-scatter.2.cloned.1.call-update) | async-done | bytes 73744 | tf_op jit(solution)/shard_map/reduce_scatter | solution.py:99
  136.0 1.6 %multiply_convert_fusion.1 = bf16[8,2304]{1,0:T(8,128)(2,1)} fusion(f32[8,2304]{1,0:T(8,128)} %reduce-scatter.2.cloned.1.call-done, f32[2304]{0:T(1024)S(1)} %convert_multiply_fusion.4, f32[8]{0:T(128)S(1)} %add_rsqrt_fusion), kind=kLoop, calls=%fused_computation.80 | loop fusion | flops 55296 | bytes 119840 | tf_op jit(solution)/shard_map/convert_element_type | solution.py:111
  (23 shorter events, 0.2 us)
Async XLA Ops:
  7.2 38.6 %copy-start = (bf16[2,4096]{1,0:T(2,128)(2,1)S(1)}, bf16[2,4096]{1,0:T(2,128)(2,1)}, u32[]{:S(2)}) copy-start(bf16[2,4096]{1,0:T(2,128)(2,1)} %param.14) | copy-start | bytes 49156
  7.2 69.7 %copy-start.2 = (bf16[4096]{0:T(1024)(128)(2,1)S(1)}, bf16[4096]{0:T(1024)(128)(2,1)}, u32[]{:S(2)}) copy-start(bf16[4096]{0:T(1024)(128)(2,1)} %param.15) | copy-start | bytes 24580
  7.2 69.7 %copy-start.1 = (s32[4096]{0:T(1024)S(1)}, s32[4096]{0:T(1024)}, u32[]{:S(2)}) copy-start(s32[4096]{0:T(1024)} %param.13) | copy-start | bytes 49156
  7.2 111.2 %all-reduce.2.cloned.1.call-start = ((), (), s32[]{:S(2)}) async-start(), calls=%async_computation.1 | async-start | bytes 524288 | tf_op jit(solution)/shard_map/psum | solution.py:91
  11.3 6.5 %collective-permute-start = (f32[8,4096]{1,0:T(8,128)S(1)}, f32[8,4096]{1,0:T(8,128)S(1)}, u32[]{:S(2)}, u32[]{:S(2)}) collective-permute-start(f32[8,4096]{1,0:T(8,128)S(1)} %reshape.16), channel_id=1, source_target_pairs={{0,2},{2,0},{4,6},{6,4},{8,10},{10,8},{12,14},{14,12},{1,3},{3,1},... | collective-permute-start | bytes 393224 | tf_op jit(solution)/shard_map/ppermute | solution.py:18
  17.8 5.0 %collective-permute-start.1 = (f32[8,4096]{1,0:T(8,128)S(1)}, f32[8,4096]{1,0:T(8,128)S(1)}, u32[]{:S(2)}, u32[]{:S(2)}) collective-permute-start(f32[8,4096]{1,0:T(8,128)S(1)} %add_select_fusion.1), channel_id=1, source_target_pairs={{0,4},{4,0},{2,6},{6,2},{8,12},{12,8},{10,14},{14,10},{1,5},{5,1},... | collective-permute-start | bytes 393224 | tf_op jit(solution)/shard_map/ppermute | solution.py:18
  22.9 7.3 %collective-permute-start.2 = (f32[8,4096]{1,0:T(8,128)S(1)}, f32[8,4096]{1,0:T(8,128)S(1)}, u32[]{:S(2)}, u32[]{:S(2)}) collective-permute-start(f32[8,4096]{1,0:T(8,128)S(1)} %add_select_fusion), channel_id=1, source_target_pairs={{0,8},{8,0},{2,10},{10,2},{4,12},{12,4},{6,14},{14,6},{1,9},{9,1},... | collective-permute-start | bytes 393224 | tf_op jit(solution)/shard_map/ppermute | solution.py:18
  45.7 90.3 %reduce-scatter.2.cloned.1.call-start = ((), (), s32[]{:S(2)}) async-start(), calls=%async_computation.2 | async-start | bytes 221184 | tf_op jit(solution)/shard_map/reduce_scatter | solution.py:99
Sparse Core Ops, SparseCore 0:
  45.8 72.5 all-reduce.1
  129.2 6.8 reduce-scatter.1
where the time goes:
time: 145 us; the launch traced here: 144 us
  waiting for transfers between devices  55.6 us (38%)
  blocking collectives  35.5 us (24%)
  matrix products  24.9 us (17%)
  between operations  14.2 us (10%)
  starting transfers between devices  7.91 us (5%)
  other arithmetic  5.27 us (4%)
    psum x1, waiting for transfers between devices, body(): summed = lax.psum(partial_value, 'hid')  41.4 us
    all_gather x1, blocking collectives, body(): every_residual = lax.all_gather(residual, 'hid', axis=0, tiled=True)  31.1 us
    dot_general x1, matrix products, body(): jnp.dot(lax.all_gather(rotated, 'row', axis=0, tiled=True), down_codes, p...  13.5 us
    ppermute x3, waiting for transfers between devices, partner_2(): return lax.ppermute(block, axis, route)  10.4 us
    dot_general x1, matrix products, body(): jnp.dot(scaled_rows, qkv_codes, preferred_element_type=jnp.float32)  9.57 us
    ppermute x3, starting transfers between devices, partner_2(): return lax.ppermute(block, axis, route)  7.83 us
    reduce_scatter x1, waiting for transfers between devices, body(): lax.psum_scatter(jnp.dot(scaled_rows, qkv_codes, preferred_element_type=j...  3.79 us
  transfers between devices with their start and end apart: 5, of which 5 were waited for; matrix products, arithmetic and copies ran while one was open for 1% of the time, Pallas kernels for 0%

commit v1 on v0

v1 whole, which is shorter than its diff:
```python
import functools
import math

import jax
import jax.numpy as jnp
from jax import lax
from jax.experimental import pallas as pl
from jax.experimental.pallas import tpu as pltpu
from jax.sharding import PartitionSpec as P

epsilon = 1e-05
F32 = jnp.float32
BF16 = jnp.bfloat16
MESH = pl.DeviceIdType.MESH


def each(count, step, start=0):
    if count - start <= 16:
        for index in range(start, count):
            step(index)
    else:

        def looped(index, carry):
            step(index)
            return carry

        lax.fori_loop(start, count, looped, 0)


def loop(count, step):
    def looped(index, carry):
        step(index)
        return carry

    lax.fori_loop(0, count, looped, 0)


def sylvester(order):
    both = lax.broadcasted_iota(jnp.int32, (order, order), 0) & lax.broadcasted_iota(
        jnp.int32, (order, order), 1
    )
    shift = 1
    while shift < order.bit_length():
        shift *= 2
    while shift > 1:
        shift //= 2
        both = both ^ lax.shift_right_logical(both, shift)
    return (1 - 2 * (both & 1)).astype(F32).astype(BF16)


def tile_of(width, largest):
    tile = largest // 128 * 128
    while width % tile:
        tile -= 128
    return tile


def kernel(
    A, B, J, width_total,
    gate_h, up_h, signs_h, wd_h, dscale_h, res_h, gain_h, wq_h, qscale_h,
    ns_o, out_o,
    gate, up, signs, dscale, res, gain, qscale, wd, wq,
    send1, recv1, xf, send2, recv2, lhsf, lhs, send3, recv3, send4, recv4, rowsf, lhs2, sq, proj,
    send5, recv5,
    in_sem, wd_sem, wq_sem, s1, r1, s2, r2, s3, r3, s4, r4, s5, r5,
):
    h = lax.axis_index("hid")
    r = lax.axis_index("row")
    N = A * B
    me = h * B + r
    Rl, FFl = gate.shape
    q = Rl // A
    R = Rl * B
    S = R // A
    C = wd.shape[2]
    Q = wq.shape[2]

    small = [
        pltpu.make_async_copy(src, dst, in_sem.at[k])
        for k, (src, dst) in enumerate(
            [(gate_h, gate), (up_h, up), (signs_h, signs), (dscale_h, dscale), (res_h, res),
             (gain_h, gain), (qscale_h, qscale)]
        )
    ]
    for copy in small:
        copy.start()

    def wd_copy(j):
        return pltpu.make_async_copy(
            wd_h.at[:, pl.ds(pl.multiple_of(j * C, C), C)], wd.at[j], wd_sem.at[j]
        )

    def wq_copy(j):
        return pltpu.make_async_copy(
            wq_h.at[pl.ds(pl.multiple_of(j * C, C), C), :], wq.at[j], wq_sem.at[j]
        )

    for j in range(J):
        wd_copy(j).start()
    for j in range(J):
        wq_copy(j).start()

    barrier = pltpu.get_barrier_semaphore()

    def greet(t):
        peer = lax.rem(me + t, N)
        pl.semaphore_signal(
            barrier, inc=1, device_id={"hid": lax.div(peer, B), "row": lax.rem(peer, B)},
            device_id_type=MESH,
        )

    each(N, greet, 1)

    for copy in small[:3]:
        copy.wait()
    v = gate[...].astype(F32)
    hidden = (v / (1.0 + jnp.exp(-v)) * up[...].astype(F32)).astype(BF16).astype(F32)
    signed = hidden * (1 - 2 * signs[...]).astype(F32)
    for a in range(A):
        send1[a] = signed[a * q:(a + 1) * q, :].astype(BF16)
    recv1[h] = send1[h]
    pl.semaphore_wait(barrier, N - 1)

    def copy1(t):
        d = lax.rem(h + t, A)
        return pltpu.make_async_remote_copy(
            src_ref=send1.at[d], dst_ref=recv1.at[h], send_sem=s1.at[t - 1], recv_sem=r1.at[t - 1],
            device_id={"hid": d}, device_id_type=MESH,
        )

    each(A, lambda t: copy1(t).start(), 1)
    W = 256
    pieces = FFl // W
    order_right = sylvester(W)
    order_left = sylvester(A * pieces)
    for copy in small[3:]:
        copy.wait()
    each(A, lambda t: copy1(t).wait(), 1)

    for k in range(q):
        for a in range(A):
            xf[a:a + 1, :] = recv1[a, k:k + 1, :].astype(F32)
        stacked = jnp.concatenate(
            [xf[:, p * W:(p + 1) * W] for p in range(pieces)], axis=0
        ).astype(BF16)
        right = jnp.dot(stacked, order_right, preferred_element_type=F32)
        top = right.astype(BF16)
        rest = right - top.astype(F32)
        middle = rest.astype(BF16)
        low = (rest - middle.astype(F32)).astype(BF16)
        both = (
            jnp.dot(order_left, low, preferred_element_type=F32)
            + jnp.dot(order_left, middle, preferred_element_type=F32)
        ) + jnp.dot(order_left, top, preferred_element_type=F32)
        both = both * (1.0 / math.sqrt(FFl * A))
        for p in range(pieces):
            xf[:, p * W:(p + 1) * W] = both[p * A:(p + 1) * A, :]
        for a in range(A):
            send2[a, k:k + 1, :] = xf[a:a + 1, :].astype(BF16)
    recv2[me] = send2[h]

    def copy2(t):
        peer = lax.rem(me + t, N)
        d = lax.div(peer, B)
        return pltpu.make_async_remote_copy(
            src_ref=send2.at[d], dst_ref=recv2.at[me], send_sem=s2.at[t - 1],
            recv_sem=r2.at[t - 1], device_id={"hid": d, "row": lax.rem(peer, B)},
            device_id_type=MESH,
        )

    each(N, lambda t: copy2(t).start(), 1)
    each(N, lambda t: copy2(t).wait(), 1)

    for b in range(B):
        for a in range(A):
            row = b * Rl + a * q
            lhsf[row:row + q, :] = recv2[a * B + b].astype(F32)
    lhs[...] = lhsf[...].astype(BF16)

    def copy3(t, j):
        d = lax.rem(h + t, A)
        return pltpu.make_async_remote_copy(
            src_ref=send3.at[j, d], dst_ref=recv3.at[j, h], send_sem=s3.at[t - 1, j],
            recv_sem=r3.at[t - 1, j], device_id={"hid": d}, device_id_type=MESH,
        )

    def copy4(t, j):
        d = lax.rem(h + t, A)
        return pltpu.make_async_remote_copy(
            src_ref=send4.at[j], dst_ref=recv4.at[j, h], send_sem=s4.at[t - 1, j],
            recv_sem=r4.at[t - 1, j], device_id={"hid": d}, device_id_type=MESH,
        )

    tile = tile_of(C, 512)

    def down_step(j):
        wd_copy(j).wait()
        for n in range(0, C, tile):
            part = jnp.dot(lhs[...], wd[j, :, n:n + tile], preferred_element_type=F32)
            for a in range(A):
                send3[j, a, :, n:n + tile] = part[a * S:(a + 1) * S, :].astype(BF16)
        recv3[j, h] = send3[j, h]
        each(A, lambda t: copy3(t, j).start(), 1)

    loop(J, down_step)

    def stream_step(j):
        each(A, lambda t: copy3(t, j).wait(), 1)
        total = recv3[j, 0].astype(F32)
        for a in range(1, A):
            total = total + recv3[j, a].astype(F32)
        columns = pl.ds(pl.multiple_of(j * C, C), C)
        total = total * (dscale[:, columns].astype(F32) * 2.0 ** (-23))
        stream = (res[:, columns].astype(F32) + total).astype(BF16)
        ns_o[:, columns] = stream
        send4[j] = stream
        recv4[j, h] = stream
        each(A, lambda t: copy4(t, j).start(), 1)

    loop(J, stream_step)

    sq[...] = jnp.zeros_like(sq)
    proj[...] = jnp.zeros_like(proj)
    tile_q = tile_of(Q, 768)

    def project_step(j):
        each(A, lambda t: copy4(t, j).wait(), 1)
        wq_copy(j).wait()
        for a in range(A):
            rowsf[a * S:(a + 1) * S, :] = recv4[j, a].astype(F32)
        wide = rowsf[...]
        columns = pl.ds(pl.multiple_of(j * C, C), C)
        lhs2[...] = (wide * gain[:, columns].astype(F32)).astype(BF16)
        sq[...] += jnp.sum(wide * wide, axis=1, keepdims=True)
        for n in range(0, Q, tile_q):
            proj[:, n:n + tile_q] += jnp.dot(
                lhs2[...], wq[j, :, n:n + tile_q], preferred_element_type=F32
            )

    loop(J, project_step)

    def copy5(t):
        d = lax.rem(r + t, B)
        return pltpu.make_async_remote_copy(
            src_ref=send5.at[d], dst_ref=recv5.at[r], send_sem=s5.at[t - 1],
            recv_sem=r5.at[t - 1], device_id={"row": d}, device_id_type=MESH,
        )

    for b in range(B):
        send5[b, :, :Q] = proj[b * Rl:(b + 1) * Rl, :]
        send5[b, :, Q:] = sq[b * Rl:(b + 1) * Rl, :]
    each(B, lambda t: copy5(t).start(), 1)
    recv5[r] = send5[r]
    each(B, lambda t: copy5(t).wait(), 1)
    total = recv5[0]
    for b in range(1, B):
        total = total + recv5[b]
    inverse = lax.rsqrt(total[:, Q:Q + 1] / width_total + epsilon)
    out_o[...] = (
        total[:, :Q] * inverse * (qscale[...].astype(F32) * 2.0 ** (-22))
    ).astype(BF16)


def body(gate, up, signs, wd, dscale, res, gain, wq, qscale):
    A = lax.axis_size("hid")
    B = lax.axis_size("row")
    N = A * B
    Rl, FFl = gate.shape
    Dl = wd.shape[1]
    Q = wq.shape[1]
    R = Rl * B
    S = res.shape[0]
    q = Rl // A
    J = 4
    C = Dl // J
    any_spec = pl.BlockSpec(memory_space=pl.ANY)
    vmem_spec = pl.BlockSpec(memory_space=pltpu.VMEM)
    dma = pltpu.SemaphoreType.DMA
    call = pl.pallas_call(
        functools.partial(kernel, A, B, J, Dl * B),
        out_shape=(
            jax.ShapeDtypeStruct((S, Dl), BF16),
            jax.ShapeDtypeStruct((Rl, Q), BF16),
        ),
        in_specs=[any_spec] * 9,
        out_specs=(vmem_spec, vmem_spec),
        scratch_shapes=[
            pltpu.VMEM((Rl, FFl), BF16),
            pltpu.VMEM((Rl, FFl), BF16),
            pltpu.VMEM((1, FFl), jnp.int32),
            pltpu.VMEM((1, Dl), jnp.int32),
            pltpu.VMEM((S, Dl), BF16),
            pltpu.VMEM((1, Dl), BF16),
            pltpu.VMEM((1, Q), jnp.int32),
            pltpu.VMEM((J, FFl, C), BF16),
            pltpu.VMEM((J, C, Q), BF16),
            pltpu.VMEM((A, q, FFl), BF16),
            pltpu.VMEM((A, q, FFl), BF16),
            pltpu.VMEM((A, FFl), F32),
            pltpu.VMEM((A, q, FFl), BF16),
            pltpu.VMEM((N, q, FFl), BF16),
            pltpu.VMEM((R, FFl), F32),
            pltpu.VMEM((R, FFl), BF16),
            pltpu.VMEM((J, A, S, C), BF16),
            pltpu.VMEM((J, A, S, C), BF16),
            pltpu.VMEM((J, S, C), BF16),
            pltpu.VMEM((J, A, S, C), BF16),
            pltpu.VMEM((R, C), F32),
            pltpu.VMEM((R, C), BF16),
            pltpu.VMEM((R, 128), F32),
            pltpu.VMEM((R, Q), F32),
            pltpu.VMEM((B, Rl, Q + 128), F32),
            pltpu.VMEM((B, Rl, Q + 128), F32),
            dma((7,)),
            dma((J,)),
            dma((J,)),
            dma((A - 1,)),
            dma((A - 1,)),
            dma((N - 1,)),
            dma((N - 1,)),
            dma((A - 1, J)),
            dma((A - 1, J)),
            dma((A - 1, J)),
            dma((A - 1, J)),
            dma((B - 1,)),
            dma((B - 1,)),
        ],
        compiler_params=pltpu.CompilerParams(
            collective_id=0, has_side_effects=True, vmem_limit_bytes=63 * 1024 * 1024
        ),
    )
    return call(
        gate, up, signs.reshape(1, -1), wd, dscale.reshape(1, -1), res, gain.reshape(1, -1), wq,
        qscale.reshape(1, -1),
    )


def solution(mesh):
    return jax.shard_map(
        body,
        mesh=mesh,
        in_specs=(
            P(("groups", "row"), "hid"),
            P(("groups", "row"), "hid"),
            P("hid"),
            P("hid", "row"),
            P("row"),
            P(("groups", "hid"), "row"),
            P("row"),
            P("row", "hid"),
            P("hid"),
        ),
        out_specs=(P(("groups", "hid"), "row"), P(("groups", "row"), "hid")),
        check_vma=False,
    )
```

time: 145 us -> 45.9 us (0.32)
  waiting for transfers between devices: 55.6 us -> 0 us
  Pallas kernels: 0 us -> 39.6 us
  blocking collectives: 35.5 us -> 0 us
  matrix products: 24.9 us -> 0 us
  between operations: 14.2 us -> 0.64 us
  starting transfers between devices: 7.91 us -> 0 us
  other arithmetic: 5.27 us -> 0 us
  local copies, waits for them, and re-layouts: 1.1 us -> 5.34 us
    psum x1 -> x0, waiting for transfers between devices: 41.4 us -> none  [body(): summed = lax.psum(partial_value, 'hid')]
    pallas_call x0 -> x1, Pallas kernels: none -> 39.6 us  [body(): call(gate, up, signs.reshape(1, -1), wd, dscale.reshape(1, -1), res, gain...]
    all_gather x2 -> x0, blocking collectives: 33 us -> none  [the longest x1 31.1 us: body(): every_residual = lax.all_gather(residual, 'hid', axis=0, tiled=True)]
    dot_general x4 -> x0, matrix products: 24.9 us -> none  [the longest x1 13.5 us: body(): jnp.dot(lax.all_gather(rotated, 'row', axis=0, tiled=True), down_codes, p...]
    ppermute x3 -> x0, waiting for transfers between devices: 10.4 us -> none  [partner_2(): return lax.ppermute(block, axis, route)]
    ppermute x3 -> x0, starting transfers between devices: 7.83 us -> none  [partner_2(): return lax.ppermute(block, axis, route)]
    reduce_scatter x1 -> x0, waiting for transfers between devices: 3.79 us -> none  [body(): lax.psum_scatter(jnp.dot(scaled_rows, qkv_codes, preferred_element_type=j...]
    unnamed x6 -> x2, local copies, waits for them, and re-layouts: 0.01 us -> 2.72 us
  transfers between devices with their start and end apart: 5 -> 0, of which waited for: 5 -> 0; matrix products, arithmetic and copies ran while one was open for 1% -> 0% of each run, Pallas kernels for 0% -> 0%
where the time goes in v1:
time: 45.9 us; the launch traced here: 45.6 us
  Pallas kernels  39.6 us (86%)
  local copies, waits for them, and re-layouts  5.34 us (12%)
  between operations  0.64 us (1%)
    pallas_call x1, Pallas kernels, body(): call(gate, up, signs.reshape(1, -1), wd, dscale.reshape(1, -1), res, gain...  39.6 us
    unnamed x2, local copies, waits for them, and re-layouts  2.72 us
    reshape x1, local copies, waits for them, and re-layouts, body(): qscale.reshape(1, -1)  1.31 us
    reshape x1, local copies, waits for them, and re-layouts, body(): gain.reshape(1, -1)  1.31 us

profile of v1, /device:TPU:0, one launch (start us, length us, event | category | flops | bytes accessed | tf_op | source)
XLA Modules:
  0.0 45.6 jit_solution(11259635593499289616)
XLA Ops:
  0.6 1.3 %reshape.19.qscale_h = s32[1,2304]{1,0:T(1,128)} reshape(s32[2304]{0:T(1024)} %param.17) | data formatting | bytes 18432 | tf_op jit(solution)/shard_map/reshape | solution.py:334
  1.9 1.3 %reshape.18.gain_h = bf16[1,4096]{1,0:T(2,128)(2,1)} reshape(bf16[4096]{0:T(1024)(128)(2,1)} %param.15) | data formatting | bytes 16384 | tf_op jit(solution)/shard_map/reshape | solution.py:333
  3.3 39.6 %shard_map.104 = (bf16[2,4096]{1,0:T(2,128)(2,1)}, bf16[8,2304]{1,0:T(8,128)(2,1)}) custom-call(bf16[8,4096]{1,0:T(8,128)(2,1)} %gate_h.1, bf16[8,4096]{1,0:T(8,128)(2,1)} %up_h.1, s32[1,4096]{1,0:T(1,128)} %bitcast.2, bf16[4096,4096]{1,0:T(8,128)(2,1)} %wd_h.1, s32[1,4096]{1,0:T(1,128)} %bitcast.3, bf16[2,4096]{1,0:T(2,128)(2,1)} %res_h.1, ...), custom_call_target="tpu_custom_call" | custom-call | tf_op jit(solution)/shard_map/pallas_call | solution.py:332
  42.8 1.3 %copy.13 = bf16[2,4096]{1,0:T(2,128)(2,1)} copy(bf16[2,4096]{1,0:T(2,128)(2,1)} %get-tuple-element.4) | data formatting | bytes 32768
  44.2 1.4 %copy.14 = bf16[8,2304]{1,0:T(8,128)(2,1)} copy(bf16[8,2304]{1,0:T(8,128)(2,1)} %get-tuple-element.5) | data formatting | bytes 73728

commit v2 on v1

--- a/solution.py
+++ b/solution.py
@@ -59,7 +59,7 @@
     A, B, J, width_total,
     gate_h, up_h, signs_h, wd_h, dscale_h, res_h, gain_h, wq_h, qscale_h,
     ns_o, out_o,
-    gate, up, signs, dscale, res, gain, qscale, wd, wq,
+    gate, up, signs, dscale, res, gain1, qscale, wd, wq, gain,
     send1, recv1, xf, send2, recv2, lhsf, lhs, send3, recv3, send4, recv4, rowsf, lhs2, sq, proj,
     send5, recv5,
     in_sem, wd_sem, wq_sem, s1, r1, s2, r2, s3, r3, s4, r4, s5, r5,
@@ -79,7 +79,7 @@
         pltpu.make_async_copy(src, dst, in_sem.at[k])
         for k, (src, dst) in enumerate(
             [(gate_h, gate), (up_h, up), (signs_h, signs), (dscale_h, dscale), (res_h, res),
-             (gain_h, gain), (qscale_h, qscale)]
+             (gain_h, gain1), (qscale_h, qscale)]
         )
     ]
     for copy in small:
@@ -96,9 +96,7 @@
         )
 
     for j in range(J):
-        wd_copy(j).start()
-    for j in range(J):
-        wq_copy(j).start()
+        wd_copy(j).start(priority=1)
 
     barrier = pltpu.get_barrier_semaphore()
 
@@ -135,6 +133,7 @@
     order_left = sylvester(A * pieces)
     for copy in small[3:]:
         copy.wait()
+    gain[...] = gain1[...].astype(F32).reshape(1, -1)
     each(A, lambda t: copy1(t).wait(), 1)
 
     for k in range(q):
@@ -171,6 +170,8 @@
     each(N, lambda t: copy2(t).start(), 1)
     each(N, lambda t: copy2(t).wait(), 1)
 
+    for j in range(J):
+        wq_copy(j).start(priority=1)
     for b in range(B):
         for a in range(A):
             row = b * Rl + a * q
@@ -230,7 +231,7 @@
             rowsf[a * S:(a + 1) * S, :] = recv4[j, a].astype(F32)
         wide = rowsf[...]
         columns = pl.ds(pl.multiple_of(j * C, C), C)
-        lhs2[...] = (wide * gain[:, columns].astype(F32)).astype(BF16)
+        lhs2[...] = (wide * gain[:, columns]).astype(BF16)
         sq[...] += jnp.sum(wide * wide, axis=1, keepdims=True)
         for n in range(0, Q, tile_q):
             proj[:, n:n + tile_q] += jnp.dot(
@@ -257,8 +258,17 @@
         total = total + recv5[b]
     inverse = lax.rsqrt(total[:, Q:Q + 1] / width_total + epsilon)
     out_o[...] = (
-        total[:, :Q] * inverse * (qscale[...].astype(F32) * 2.0 ** (-22))
+        total[:, :Q] * inverse * (qscale[...].astype(F32).reshape(1, Q) * 2.0 ** (-22))
     ).astype(BF16)
+
+
+def hand_over(ns, out, ns_o, out_o, sem):
+    first = pltpu.make_async_copy(ns, ns_o, sem.at[0])
+    second = pltpu.make_async_copy(out, out_o, sem.at[1])
+    first.start()
+    second.start()
+    first.wait()
+    second.wait()
 
 
 def body(gate, up, signs, wd, dscale, res, gain, wq, qscale):
@@ -290,10 +300,11 @@
             pltpu.VMEM((1, FFl), jnp.int32),
             pltpu.VMEM((1, Dl), jnp.int32),
             pltpu.VMEM((S, Dl), BF16),
-            pltpu.VMEM((1, Dl), BF16),
-            pltpu.VMEM((1, Q), jnp.int32),
+            pltpu.VMEM((Dl,), BF16),
+            pltpu.VMEM((Q,), jnp.int32),
             pltpu.VMEM((J, FFl, C), BF16),
             pltpu.VMEM((J, C, Q), BF16),
+            pltpu.VMEM((1, Dl), F32),
             pltpu.VMEM((A, q, FFl), BF16),
             pltpu.VMEM((A, q, FFl), BF16),
             pltpu.VMEM((A, FFl), F32),
@@ -329,10 +340,17 @@
             collective_id=0, has_side_effects=True, vmem_limit_bytes=63 * 1024 * 1024
         ),
     )
-    return call(
-        gate, up, signs.reshape(1, -1), wd, dscale.reshape(1, -1), res, gain.reshape(1, -1), wq,
-        qscale.reshape(1, -1),
+    made = call(
+        gate, up, signs.reshape(1, -1), wd, dscale.reshape(1, -1), res, gain, wq,
+        qscale,
     )
+    return pl.pallas_call(
+        hand_over,
+        out_shape=(jax.ShapeDtypeStruct((S, Dl), BF16), jax.ShapeDtypeStruct((Rl, Q), BF16)),
+        in_specs=[vmem_spec, vmem_spec],
+        out_specs=(any_spec, any_spec),
+        scratch_shapes=[dma((2,))],
+    )(*made)
 
 
 def solution(mesh):

time: 45.9 us -> 37.1 us (0.81)
  local copies, waits for them, and re-layouts: 5.34 us -> 0 us
  Pallas kernels: 39.6 us -> 36.3 us
    pallas_call x1, Pallas kernels: 39.6 us -> 34.8 us  [body(): call(gate, up, signs.reshape(1, -1), wd, dscale.reshape(1, -1), res, gain...]
    unnamed x2 -> x0, local copies, waits for them, and re-layouts: 2.72 us -> none
    reshape x2 -> x0, local copies, waits for them, and re-layouts: 2.62 us -> none  [the longest x1 1.31 us: body(): qscale.reshape(1, -1)]
    pallas_call x0 -> x1, Pallas kernels: none -> 1.42 us  [body(): pl.pallas_call(hand_over, out_shape=(jax.ShapeDtypeStruct((S, Dl), BF16),...]
where the time goes in v2:
time: 37.1 us; the launch traced here: 36.9 us
  Pallas kernels  36.3 us (98%)
  between operations  0.64 us (2%)
    pallas_call x1, Pallas kernels, body(): call(gate, up, signs.reshape(1, -1), wd, dscale.reshape(1, -1), res, gain...  34.8 us
    pallas_call x1, Pallas kernels, body(): pl.pallas_call(hand_over, out_shape=(jax.ShapeDtypeStruct((S, Dl), BF16),...  1.42 us

profile of v2, /device:TPU:0, one launch (start us, length us, event | category | flops | bytes accessed | tf_op | source)
XLA Modules:
  0.0 36.9 jit_solution(17271988377374057545)
XLA Ops:
  0.6 34.8 %shard_map.104 = (bf16[2,4096]{1,0:T(2,128)(2,1)}, bf16[8,2304]{1,0:T(8,128)(2,1)}) custom-call(bf16[8,4096]{1,0:T(8,128)(2,1)} %gate_h.1, bf16[8,4096]{1,0:T(8,128)(2,1)} %up_h.1, s32[1,4096]{1,0:T(1,128)} %bitcast.2, bf16[4096,4096]{1,0:T(8,128)(2,1)} %wd_h.1, s32[1,4096]{1,0:T(1,128)} %bitcast.3, bf16[2,4096]{1,0:T(2,128)(2,1)} %res_h.1, ...), custom_call_target="tpu_custom_call" | custom-call | tf_op jit(solution)/shard_map/pallas_call | solution.py:343
  35.5 1.4 %shard_map.105 = (bf16[2,4096]{1,0:T(2,128)(2,1)}, bf16[8,2304]{1,0:T(8,128)(2,1)}) custom-call(bf16[2,4096]{1,0:T(2,128)(2,1)} %get-tuple-element.4.ns, bf16[8,2304]{1,0:T(8,128)(2,1)} %get-tuple-element.5.out), custom_call_target="tpu_custom_call" | custom-call | tf_op jit(solution)/shard_map/pallas_call | solution.py:347
